TPU v7x, 32 devices: a whole 2x2x4 slice. The times are simulated.
32 devices in a mesh: pt: 8 (over z, y), tm: 4 (over x, core).
Axes of the slice: x: 2, y: 2, z: 4, core: 2. Of those that a mesh axis runs over, the one named last changes fastest.
Arguments:
- signals: float32 [512, 32768], P('pt', 'tm'), may hold values from -6 to 6
- freq_bins: int32 [4], replicated, may hold values from 1 to 511
Outputs:
- cross_spectra: float32 [2, 4, 512, 512], P(None, None, 'pt', 'tm')
All inputs are finite; a program needn't handle non-finite values.
Results may differ from a plain program's by a relative error of at most 0.000064.
Values sent between devices are 32-bit elements; how exact they have to be, the bound alone decides.
No kernel may reach another device: no remote copies, remote signals or barrier semaphores. Data moves between devices by JAX's collectives and lax.ppermute only.
A program may use at most 64 MiB of HBM per device.

v0:
```python
import math
import jax
import jax.numpy as jnp
from jax import lax
from jax.sharding import PartitionSpec as P

SEGLEN = 1024
TWO_PI = 2.0 * math.pi


def shifted(value, axis, steps):
    count = lax.axis_size(axis)
    initial, last = (max(0, -steps), min(count, count - steps))
    return lax.ppermute(value, axis, [(source, source + steps) for source in range(initial, last)])


def dft_tables(freq_bins, seg_len):
    sample_index = jnp.arange(seg_len, dtype=jnp.int32)
    wrapped = sample_index[:, None] * freq_bins[None, :] % seg_len
    angles = wrapped.astype(jnp.float32) * (TWO_PI / seg_len)
    window = 0.5 - 0.5 * jnp.cos(sample_index.astype(jnp.float32) * (TWO_PI / seg_len))
    cosine = window[:, None] * jnp.cos(angles)
    sine_part = -window[:, None] * jnp.sin(angles)
    full_table = jnp.concatenate([cosine, sine_part], axis=1)
    half_len = seg_len // 2
    return jnp.concatenate([full_table[:half_len], full_table[half_len:]], axis=1)


def tile_products(left_side, right_side):
    stacked_right = jnp.concatenate([right_side[:, 0], right_side[:, 1]], axis=2)
    real_left = jnp.concatenate([left_side[:, 0], left_side[:, 1]], axis=2)
    imag_left = jnp.concatenate([left_side[:, 1], -left_side[:, 0]], axis=2)
    real_part = jnp.einsum(
        "fps,fqs->fpq", real_left, stacked_right, precision=lax.Precision.HIGHEST
    )
    imag_part = jnp.einsum(
        "fps,fqs->fpq", imag_left, stacked_right, precision=lax.Precision.HIGHEST
    )
    return jnp.stack([real_part, imag_part])


def body(signals, freq_bins):
    point_rows, sample_count = signals.shape
    half_len = SEGLEN // 2
    blocks_dev = sample_count // half_len
    bin_count = freq_bins.shape[0]
    columns = 2 * bin_count
    table = dft_tables(freq_bins, SEGLEN)
    blocks = signals.reshape(point_rows, blocks_dev, half_len)
    projected = jnp.einsum("pbn,nc->pbc", blocks, table, precision=lax.Precision.HIGHEST)
    incoming = shifted(signals[:, :half_len], "tm", -1)
    boundary = jnp.dot(
        incoming,
        table[:, columns:],
        precision=lax.Precision.HIGHEST,
        preferred_element_type=jnp.float32,
    )
    following = jnp.concatenate([projected[:, 1:, columns:], boundary[:, None, :]], axis=1)
    spectra = projected[:, :, :columns] + following
    is_last = lax.axis_index("tm") == lax.axis_size("tm") - 1
    segment_ids = jnp.arange(blocks_dev, dtype=jnp.int32)
    weight_mask = jnp.where(
        jnp.logical_and(is_last, segment_ids == blocks_dev - 1), 0.0, 1.0
    ).astype(jnp.float32)
    spectra = spectra * weight_mask[None, :, None]
    spectra_panel = spectra.reshape(point_rows, blocks_dev, 2, bin_count).transpose(3, 2, 0, 1)
    partial_tiles = tile_products(
        spectra_panel, lax.all_gather(spectra_panel, "pt", axis=2, tiled=True)
    )
    summed = lax.psum_scatter(partial_tiles, "tm", scatter_dimension=3, tiled=True)
    total_segments = blocks_dev * lax.axis_size("tm") - 1
    scale = 1.0 / (total_segments * 0.375 * SEGLEN)
    return summed * scale


def solution(mesh):
    in_specs = (P("pt", "tm"), P())
    out_specs = P(None, None, "pt", "tm")
    return jax.shard_map(body, mesh=mesh, in_specs=in_specs, out_specs=out_specs, check_vma=False)
```

profile of v0, /device:TPU:0, one launch (start us, length us, event | category | flops | bytes accessed | tf_op | source)
XLA Modules:
  0.0 97.8 jit_solution(1529557021851676892)
XLA Ops:
  6.5 0.0 reduce-scatter.2.cloned.1.call-start
  6.5 0.9 slice.33
  7.5 1.3 %collective-permute-start = (f32[64,512]{1,0:T(8,128)S(1)}, f32[64,512]{1,0:T(8,128)S(1)}, u32[]{:S(2)}, u32[]{:S(2)}) collective-permute-start(f32[64,512]{1,0:T(8,128)S(1)} %slice.33), channel_id=1, source_target_pairs={{1,0},{2,1},{3,2},{5,4},{6,5},{7,6},{9,8},{10,9},{11,10},{13,12},{... | collective-permute-start | bytes 393224 | tf_op jit(solution)/shard_map/ppermute | solution.py:14
  8.8 0.9 cosine_multiply_fusion
  9.7 4.2 %fusion.3 = f32[64,16,16]{0,2,1:T(8,128)S(1)} fusion(f32[8,16,8,512]{3,2,1,0:T(8,128)} %bitcast.33, f32[512,8]{0,1:T(8,128)S(1)} %get-tuple-element.10, f32[512,8]{0,1:T(8,128)S(1)} %get-tuple-element.9), kind=kOutput, calls=%fused_computation.5 | convolution fusion | flops 100671488 | bytes 2195456 | tf_op jit(solution)/shard_map/pbn,nc->pbc/dot_general | solution.py:50
  13.9 0.0 collective-permute-done
  13.9 0.2 convolution_bitcast_fusion.2
  14.1 0.1 fusion.6
  14.2 0.2 copy.7
  14.4 47.1 %all_gather.3 = f32[4,2,512,16]{3,0,1,2:T(4,128)S(1)} all-gather(f32[4,2,64,16]{3,0,1,2:T(4,128)S(1)} %copy.7), channel_id=1, replica_groups=mesh['pt'=8,'tm'=4] {'pt'}, dimensions={2}, use_global_device_ids=true | all-gather | bytes 294912 | tf_op jit(solution)/shard_map/all_gather | solution.py:68
  61.5 0.4 fusion.24
  61.9 0.3 copy.10
  62.2 0.3 copy.11
  62.5 0.6 convolution_bitcast_fusion.1
  63.2 0.6 convolution_bitcast_fusion
  63.8 1.0 %pad_maximum_fusion = f32[2,4,64,512]{3,2,1,0:T(8,128)} fusion(f32[1,4,64,512]{3,2,1,0:T(8,128)S(1)} %convolution_bitcast_fusion, f32[1,4,64,512]{3,2,1,0:T(8,128)S(1)} %convolution_bitcast_fusion.1), kind=kLoop, calls=%fused_computation.7 | loop fusion | flops 262144 | bytes 2097152 | tf_op jit(solution)/shard_map/stack | solution.py:39
  64.9 0.0 reduce-scatter.2.cloned.1.call-update
  64.9 24.3 %reduce-scatter.2.cloned.1.call-done = f32[2,4,64,128]{3,2,1,0:T(8,128)} async-done(((f32[2,4,64,512]{3,2,1,0:T(8,128)}), f32[2,4,64,128]{3,2,1,0:T(8,128)}) %reduce-scatter.2.cloned.1.call-update) | async-done | bytes 262160 | tf_op jit(solution)/shard_map/reduce_scatter | solution.py:70
  89.2 1.7 %broadcast_multiply_fusion = f32[2,4,64,128]{3,2,1,0:T(8,128)} fusion(f32[2,4,64,128]{3,2,1,0:T(8,128)} %reduce-scatter.2.cloned.1.call-done), kind=kLoop, calls=%fused_computation.9 | loop fusion | flops 65536 | bytes 524288 | tf_op jit(solution)/shard_map/mul | solution.py:73
  (7 shorter events, 0.1 us)
Async XLA Ops:
  6.5 82.7 %reduce-scatter.2.cloned.1.call-start = ((), (), s32[]{:S(2)}) async-start(), calls=%async_computation.1 | async-start | bytes 1310720 | tf_op jit(solution)/shard_map/reduce_scatter | solution.py:70
  7.5 6.4 %collective-permute-start = (f32[64,512]{1,0:T(8,128)S(1)}, f32[64,512]{1,0:T(8,128)S(1)}, u32[]{:S(2)}, u32[]{:S(2)}) collective-permute-start(f32[64,512]{1,0:T(8,128)S(1)} %slice.33), channel_id=1, source_target_pairs={{1,0},{2,1},{3,2},{5,4},{6,5},{7,6},{9,8},{10,9},{11,10},{13,12},{... | collective-permute-start | bytes 393224 | tf_op jit(solution)/shard_map/ppermute | solution.py:14
Sparse Core Ops, SparseCore 0:
  65.0 24.1 reduce-scatter.1
where the time goes:
time: 98 us; the launch traced here: 97.8 us
  blocking collectives  47.1 us (48%)
  waiting for transfers between devices  24.4 us (25%)
  between operations  13.5 us (14%)
  matrix products  5.6 us (6%)
  other arithmetic  3.79 us (4%)
  local copies, waits for them, and re-layouts  2.13 us (2%)
  starting transfers between devices  1.29 us (1%)
    all_gather x1, blocking collectives, body(): lax.all_gather(spectra_panel, 'pt', axis=2, tiled=True)  47.1 us
    reduce_scatter x1, waiting for transfers between devices, body(): lax.psum_scatter(partial_tiles, 'tm', scatter_dimension=3, tiled=True)  24.3 us
    dot_general x1, matrix products, body(): jnp.einsum('pbn,nc->pbc', blocks, table, precision=lax.Precision.HIGHEST)  4.15 us
  transfers between devices with their start and end apart: 2, of which 1 were waited for; matrix products, arithmetic and copies ran while one was open for 5% of the time, Pallas kernels for 0%

commit v1 on v0

--- a/solution.py
+++ b/solution.py
@@ -6,6 +6,29 @@
 
 SEGLEN = 1024
 TWO_PI = 2.0 * math.pi
+
+
+def laid_out(tiles, dim):
+    tiles = jnp.moveaxis(tiles, 0, dim)
+    dims = tiles.shape
+    return tiles.reshape(*dims[:dim], dims[dim] * dims[dim + 1], *dims[dim + 2 :])
+
+
+def doubled(x, axis):
+    size, index = (lax.axis_size(axis), lax.axis_index(axis))
+    parts, apart = (x[None], 1)
+    while apart < size:
+        partner_block = lax.ppermute(parts, axis, [(i, i ^ apart) for i in range(size)])
+        low = index & apart == 0
+        parts = jnp.concatenate(
+            [jnp.where(low, parts, partner_block), jnp.where(low, partner_block, parts)]
+        )
+        apart *= 2
+    return parts
+
+
+def doubled_up(x, axis, dim):
+    return laid_out(doubled(x, axis), dim)
 
 
 def shifted(value, axis, steps):
@@ -64,9 +87,7 @@
     ).astype(jnp.float32)
     spectra = spectra * weight_mask[None, :, None]
     spectra_panel = spectra.reshape(point_rows, blocks_dev, 2, bin_count).transpose(3, 2, 0, 1)
-    partial_tiles = tile_products(
-        spectra_panel, lax.all_gather(spectra_panel, "pt", axis=2, tiled=True)
-    )
+    partial_tiles = tile_products(spectra_panel, doubled_up(spectra_panel, "pt", 2))
     summed = lax.psum_scatter(partial_tiles, "tm", scatter_dimension=3, tiled=True)
     total_segments = blocks_dev * lax.axis_size("tm") - 1
     scale = 1.0 / (total_segments * 0.375 * SEGLEN)

time: 98 us -> 77.6 us (0.79)
  blocking collectives: 47.1 us -> 0 us
  waiting for transfers between devices: 24.4 us -> 43.4 us
  starting transfers between devices: 1.29 us -> 9.48 us
    all_gather x1 -> x0, blocking collectives: 47.1 us -> none  [body(): lax.all_gather(spectra_panel, 'pt', axis=2, tiled=True)]
    ppermute x0 -> x3, waiting for transfers between devices: none -> 17.9 us  [doubled(): lax.ppermute(parts, axis, [(i, i ^ apart) for i in range(size)])]
    ppermute x0 -> x3, starting transfers between devices: none -> 8.19 us  [doubled(): lax.ppermute(parts, axis, [(i, i ^ apart) for i in range(size)])]
    reduce_scatter x1, waiting for transfers between devices: 24.3 us -> 25.5 us  [body(): lax.psum_scatter(partial_tiles, 'tm', scatter_dimension=3, tiled=True)]
  transfers between devices with their start and end apart: 2 -> 5, of which waited for: 1 -> 4; matrix products, arithmetic and copies ran while one was open for 5% -> 7% of each run, Pallas kernels for 0% -> 0%
where the time goes in v1:
time: 77.6 us; the launch traced here: 77.4 us
  waiting for transfers between devices  43.4 us (56%)
  between operations  13.5 us (17%)
  starting transfers between devices  9.48 us (12%)
  matrix products  5.59 us (7%)
  other arithmetic  3.95 us (5%)
  local copies, waits for them, and re-layouts  1.41 us (2%)
    reduce_scatter x1, waiting for transfers between devices, body(): lax.psum_scatter(partial_tiles, 'tm', scatter_dimension=3, tiled=True)  25.5 us
    ppermute x3, waiting for transfers between devices, doubled(): lax.ppermute(parts, axis, [(i, i ^ apart) for i in range(size)])  17.9 us
    ppermute x3, starting transfers between devices, doubled(): lax.ppermute(parts, axis, [(i, i ^ apart) for i in range(size)])  8.19 us
    dot_general x1, matrix products, body(): jnp.einsum('pbn,nc->pbc', blocks, table, precision=lax.Precision.HIGHEST)  4.15 us
    mul x1, other arithmetic, body(): return summed * scale  1.68 us
  transfers between devices with their start and end apart: 5, of which 4 were waited for; matrix products, arithmetic and copies ran while one was open for 7% of the time, Pallas kernels for 0%

profile of v1, /device:TPU:0, one launch (start us, length us, event | category | flops | bytes accessed | tf_op | source)
XLA Modules:
  0.0 77.4 jit_solution(10008782146363431330)
XLA Ops:
  6.5 0.0 reduce-scatter.2.cloned.1.call-start
  6.5 0.9 %slice.33 = f32[64,512]{1,0:T(8,128)S(1)} slice(f32[64,8192]{1,0:T(8,128)} %param.2), slice={[0:64], [0:512]} | slice | bytes 262144 | tf_op jit(solution)/shard_map/slice | solution.py:74
  7.5 1.3 %collective-permute-start = (f32[64,512]{1,0:T(8,128)S(1)}, f32[64,512]{1,0:T(8,128)S(1)}, u32[]{:S(2)}, u32[]{:S(2)}) collective-permute-start(f32[64,512]{1,0:T(8,128)S(1)} %slice.33), channel_id=1, source_target_pairs={{1,0},{2,1},{3,2},{5,4},{6,5},{7,6},{9,8},{10,9},{11,10},{13,12},{... | collective-permute-start | bytes 393224 | tf_op jit(solution)/shard_map/ppermute | solution.py:37
  8.8 0.9 %cosine_multiply_fusion = (f32[1024,4]{0,1:T(4,128)S(1)}, f32[1024,4]{0,1:T(4,128)S(1)}) fusion(s32[4]{0:T(128)} %param.3, f32[1024]{0:T(1024)S(1)} %get-tuple-element.21, f32[1024]{0:T(1024)S(1)} %get-tuple-element.22), kind=kLoop, calls=%fused_computation.47 | loop fusion | flops 65536 | bytes 40976 | tf_op jit(solution)/shard_map/mul | solution.py:45
  9.7 4.2 %fusion.3 = f32[64,16,16]{0,2,1:T(8,128)S(1)} fusion(f32[8,16,8,512]{3,2,1,0:T(8,128)} %bitcast.48, f32[512,8]{0,1:T(8,128)S(1)} %get-tuple-element.18, f32[512,8]{0,1:T(8,128)S(1)} %get-tuple-element.17), kind=kOutput, calls=%fused_computation.5 | convolution fusion | flops 100671488 | bytes 2195456 | tf_op jit(solution)/shard_map/pbn,nc->pbc/dot_general | solution.py:73
  13.9 0.0 collective-permute-done
  13.9 0.2 convolution_bitcast_fusion.2
  14.1 0.1 fusion.6
  14.2 3.0 %collective-permute-start.1 = (f32[1,4,2,64,16]{3,4,1,2,0:T(8,128)S(1)}, f32[1,4,2,64,16]{3,4,1,2,0:T(8,128)S(1)}, u32[]{:S(2)}, u32[]{:S(2)}) collective-permute-start(f32[1,4,2,64,16]{3,4,1,2,0:T(8,128)S(1)} %bitcast.51), channel_id=1, source_target_pairs={{0,4},{4,0},{8,12},{12,8},{16,20},{20,16},{24,28},{28,24},{1,5},{5... | collective-permute-start | bytes 98312 | tf_op jit(solution)/shard_map/ppermute | solution.py:21
  17.3 2.6 %collective-permute-done.1 = f32[1,4,2,64,16]{3,4,1,2,0:T(8,128)S(1)} collective-permute-done((f32[1,4,2,64,16]{3,4,1,2,0:T(8,128)S(1)}, f32[1,4,2,64,16]{3,4,1,2,0:T(8,128)S(1)}, u32[]{:S(2)}, u32[]{:S(2)}) %collective-permute-start.1) | collective-permute-done | bytes 32800 | tf_op jit(solution)/shard_map/ppermute | solution.py:21
  19.9 2.3 %collective-permute-start.2 = (f32[2,4,2,64,16]{3,4,1,2,0:T(8,128)S(1)}, f32[2,4,2,64,16]{3,4,1,2,0:T(8,128)S(1)}, u32[]{:S(2)}, u32[]{:S(2)}) collective-permute-start(f32[2,4,2,64,16]{3,4,1,2,0:T(8,128)S(1)} %pad_maximum_fusion.5), channel_id=1, source_target_pairs={{0,8},{4,12},{8,0},{12,4},{16,24},{20,28},{24,16},{28,20},{1,9},{5... | collective-permute-start | bytes 196616 | tf_op jit(solution)/shard_map/ppermute | solution.py:21
  22.2 3.8 %collective-permute-done.2 = f32[2,4,2,64,16]{3,4,1,2,0:T(8,128)S(1)} collective-permute-done((f32[2,4,2,64,16]{3,4,1,2,0:T(8,128)S(1)}, f32[2,4,2,64,16]{3,4,1,2,0:T(8,128)S(1)}, u32[]{:S(2)}, u32[]{:S(2)}) %collective-permute-start.2) | collective-permute-done | bytes 65568 | tf_op jit(solution)/shard_map/ppermute | solution.py:21
  26.1 2.8 %collective-permute-start.3 = (f32[4,4,2,64,16]{3,4,1,2,0:T(8,128)S(1)}, f32[4,4,2,64,16]{3,4,1,2,0:T(8,128)S(1)}, u32[]{:S(2)}, u32[]{:S(2)}) collective-permute-start(f32[4,4,2,64,16]{3,4,1,2,0:T(8,128)S(1)} %pad_maximum_fusion.1), channel_id=1, source_target_pairs={{0,16},{4,20},{8,24},{12,28},{16,0},{20,4},{24,8},{28,12},{1,17},{... | collective-permute-start | bytes 393224 | tf_op jit(solution)/shard_map/ppermute | solution.py:21
  28.9 11.6 %collective-permute-done.3 = f32[4,4,2,64,16]{3,4,1,2,0:T(8,128)S(1)} collective-permute-done((f32[4,4,2,64,16]{3,4,1,2,0:T(8,128)S(1)}, f32[4,4,2,64,16]{3,4,1,2,0:T(8,128)S(1)}, u32[]{:S(2)}, u32[]{:S(2)}) %collective-permute-start.3) | collective-permute-done | bytes 131104 | tf_op jit(solution)/shard_map/ppermute | solution.py:21
  40.6 0.3 copy.5
  40.9 0.1 reshape.30
  41.1 0.6 convolution_bitcast_fusion
  41.7 0.6 convolution_bitcast_fusion.1
  42.3 1.0 %pad_maximum_fusion = f32[2,4,64,512]{3,2,1,0:T(8,128)} fusion(f32[1,4,64,512]{3,2,1,0:T(8,128)S(1)} %convolution_bitcast_fusion, f32[1,4,64,512]{3,2,1,0:T(8,128)S(1)} %convolution_bitcast_fusion.1), kind=kLoop, calls=%fused_computation.7 | loop fusion | flops 262144 | bytes 2097152 | tf_op jit(solution)/shard_map/stack | solution.py:62
  43.4 0.0 reduce-scatter.2.cloned.1.call-update
  43.4 25.5 %reduce-scatter.2.cloned.1.call-done = f32[2,4,64,128]{3,2,1,0:T(8,128)} async-done(((f32[2,4,64,512]{3,2,1,0:T(8,128)}), f32[2,4,64,128]{3,2,1,0:T(8,128)}) %reduce-scatter.2.cloned.1.call-update) | async-done | bytes 262160 | tf_op jit(solution)/shard_map/reduce_scatter | solution.py:91
  68.9 1.7 %broadcast_multiply_fusion = f32[2,4,64,128]{3,2,1,0:T(8,128)} fusion(f32[2,4,64,128]{3,2,1,0:T(8,128)} %reduce-scatter.2.cloned.1.call-done), kind=kLoop, calls=%fused_computation.14 | loop fusion | flops 65536 | bytes 524288 | tf_op jit(solution)/shard_map/mul | solution.py:94
  (14 shorter events, 0.3 us)
Async XLA Ops:
  6.5 62.4 %reduce-scatter.2.cloned.1.call-start = ((), (), s32[]{:S(2)}) async-start(), calls=%async_computation.1 | async-start | bytes 1310720 | tf_op jit(solution)/shard_map/reduce_scatter | solution.py:91
  7.5 6.4 %collective-permute-start = (f32[64,512]{1,0:T(8,128)S(1)}, f32[64,512]{1,0:T(8,128)S(1)}, u32[]{:S(2)}, u32[]{:S(2)}) collective-permute-start(f32[64,512]{1,0:T(8,128)S(1)} %slice.33), channel_id=1, source_target_pairs={{1,0},{2,1},{3,2},{5,4},{6,5},{7,6},{9,8},{10,9},{11,10},{13,12},{... | collective-permute-start | bytes 393224 | tf_op jit(solution)/shard_map/ppermute | solution.py:37
  14.2 5.6 %collective-permute-start.1 = (f32[1,4,2,64,16]{3,4,1,2,0:T(8,128)S(1)}, f32[1,4,2,64,16]{3,4,1,2,0:T(8,128)S(1)}, u32[]{:S(2)}, u32[]{:S(2)}) collective-permute-start(f32[1,4,2,64,16]{3,4,1,2,0:T(8,128)S(1)} %bitcast.51), channel_id=1, source_target_pairs={{0,4},{4,0},{8,12},{12,8},{16,20},{20,16},{24,28},{28,24},{1,5},{5... | collective-permute-start | bytes 98312 | tf_op jit(solution)/shard_map/ppermute | solution.py:21
  19.9 6.1 %collective-permute-start.2 = (f32[2,4,2,64,16]{3,4,1,2,0:T(8,128)S(1)}, f32[2,4,2,64,16]{3,4,1,2,0:T(8,128)S(1)}, u32[]{:S(2)}, u32[]{:S(2)}) collective-permute-start(f32[2,4,2,64,16]{3,4,1,2,0:T(8,128)S(1)} %pad_maximum_fusion.5), channel_id=1, source_target_pairs={{0,8},{4,12},{8,0},{12,4},{16,24},{20,28},{24,16},{28,20},{1,9},{5... | collective-permute-start | bytes 196616 | tf_op jit(solution)/shard_map/ppermute | solution.py:21
  26.1 14.4 %collective-permute-start.3 = (f32[4,4,2,64,16]{3,4,1,2,0:T(8,128)S(1)}, f32[4,4,2,64,16]{3,4,1,2,0:T(8,128)S(1)}, u32[]{:S(2)}, u32[]{:S(2)}) collective-permute-start(f32[4,4,2,64,16]{3,4,1,2,0:T(8,128)S(1)} %pad_maximum_fusion.1), channel_id=1, source_target_pairs={{0,16},{4,20},{8,24},{12,28},{16,0},{20,4},{24,8},{28,12},{1,17},{... | collective-permute-start | bytes 393224 | tf_op jit(solution)/shard_map/ppermute | solution.py:21
Sparse Core Ops, SparseCore 0:
  43.5 25.3 reduce-scatter.1
